TPU v7x, 512 devices: a whole 4x4x16 slice. The times are simulated.
512 devices in a mesh: req: 64 (over z, y), tp: 8 (over x, core).
Axes of the slice: x: 4, y: 4, z: 16, core: 2. Of those that a mesh axis runs over, the one named last changes fastest.
Arguments:
- hidden_in: bfloat16 [1024, 2048], P('req'), may hold values from -6 to 6
- query: bfloat16 [1024, 2048], P('req', 'tp'), may hold values from -200 to 200
- new_kv: bfloat16 [1024, 4096], P('req', 'tp'), may hold values from -6 to 6
- pool_cache: bfloat16 [5120, 32, 4096], P('req', None, 'tp'), may hold values from -7 to 7
- prompt_table: int32 [128, 24], P('req'), may hold values from 0 to 79, as said below
- prompt_len: int32 [128], P('req'), may hold values from 32 to 768
- req_group: int32 [1024], P('req'), may hold values from 0 to 1, as said below
- cont_table: int32 [1024, 2], P('req'), may hold values from 0 to 79, as said below
- cont_len: int32 [1024], P('req'), may hold values from 1 to 63
- migration: int32 [384, 2], P('req'), may hold values from 0 to 15, as said below
- diff_lambda: float32 [8], P('tp'), may hold values from 0.2 to 0.8
- out_weight: bfloat16 [2048, 2048], P('tp'), may hold values from -0.125 to 0.125
- norm_gain: float32 [2048], replicated, may hold values from 0.1 to 1.9
Outputs:
- hidden_out: bfloat16 [1024, 2048], P('req')
- normed_out: bfloat16 [1024, 2048], P('req')
- arrived: bfloat16 [512, 64, 4096], P('req', None, 'tp')
Inputs may be any that keep to these rules, and one draw needn't show every extreme that they name: `prompt_table`: entries are pages local to the row's index of req; with cont_table, each of a device's 80 pages appears exactly once. `cont_table`: local pages, each page of a device once together with prompt_table. `req_group`: A group index local to the device; every group of a device has a request. `migration`: each device lists 6 rows: a distinct local request slot and a destination offset 1 to 4 along req (with wrap); at most 2 rows of a device share an offset, and that many is reached.
All inputs are finite; a program needn't handle non-finite values.
Results may differ from a plain program's by a relative error of at most 0.012.
Values may be sent and summed in bfloat16 or wider, within the bound.
A program may use at most 64 MiB of HBM per device.

v0:
```python
import jax
import jax.numpy as jnp
from jax import lax
from jax.sharding import PartitionSpec as P

MIG_REACH = 4
MIG_CAP = 2


def shifted(value, axis, steps):
    count = lax.axis_size(axis)
    pairs = [(source, (source + steps) % count) for source in range(count)]
    return lax.ppermute(value, axis, pairs)


def head_attention(
    queries,
    new_rows,
    page_pool,
    prompt_table,
    prompt_len,
    req_group,
    cont_table,
    cont_len,
    diff_lambda,
):
    row_count = queries.shape[0]
    head_count = diff_lambda.shape[0]
    head_width = page_pool.shape[-1] // head_count
    key_width = queries.shape[-1] // head_count // 2
    value_width = head_width - 2 * key_width
    page_len = page_pool.shape[1]
    group_count = prompt_table.shape[0]
    page_of = jnp.take_along_axis(cont_table, (cont_len // page_len)[:, None], axis=1)[:, 0]
    page_pool = page_pool.at[page_of, cont_len % page_len].set(new_rows)
    prompt_keys = page_pool[prompt_table].reshape(group_count, -1, head_count, head_width)
    cont_keys = page_pool[cont_table].reshape(row_count, -1, head_count, head_width)
    split_query = queries.reshape(row_count, head_count, 2, key_width)
    prompt_pos = jnp.arange(prompt_keys.shape[1], dtype=jnp.int32)
    cont_pos = jnp.arange(cont_keys.shape[1], dtype=jnp.int32)
    group_ids = jnp.arange(group_count, dtype=jnp.int32)
    prompt_mask = (req_group[:, None, None] == group_ids[None, :, None]) & (
        prompt_pos[None, None, :] < prompt_len[None, :, None]
    )
    prompt_mask = prompt_mask[:, None]
    cont_mask = (cont_pos[None, :] <= cont_len[:, None])[:, None]
    score_scale = key_width ** (-0.5)
    prompt_values = prompt_keys[..., 2 * key_width :]
    cont_values = cont_keys[..., 2 * key_width :]
    outputs = []
    for twin_map in range(2):
        start_col = twin_map * key_width
        prompt_score = (
            jnp.einsum(
                "rhd,gjhd->rhgj",
                split_query[:, :, twin_map],
                prompt_keys[..., start_col : start_col + key_width],
                preferred_element_type=jnp.float32,
            )
            * score_scale
        )
        cont_score = (
            jnp.einsum(
                "rhd,rjhd->rhj",
                split_query[:, :, twin_map],
                cont_keys[..., start_col : start_col + key_width],
                preferred_element_type=jnp.float32,
            )
            * score_scale
        )
        prompt_score = jnp.where(prompt_mask, prompt_score, -1e30)
        cont_score = jnp.where(cont_mask, cont_score, -1e30)
        top_score = jnp.maximum(prompt_score.max(axis=(2, 3)), cont_score.max(axis=2))
        prompt_exp = jnp.exp(prompt_score - top_score[:, :, None, None])
        cont_exp = jnp.exp(cont_score - top_score[:, :, None])
        denominator = prompt_exp.sum(axis=(2, 3)) + cont_exp.sum(axis=2)
        prompt_weight = (prompt_exp / denominator[:, :, None, None]).astype(jnp.bfloat16)
        cont_weight = (cont_exp / denominator[:, :, None]).astype(jnp.bfloat16)
        mixture = jnp.einsum(
            "rhgj,gjhe->rhe", prompt_weight, prompt_values, preferred_element_type=jnp.float32
        )
        mixture = mixture + jnp.einsum(
            "rhj,rjhe->rhe", cont_weight, cont_values, preferred_element_type=jnp.float32
        )
        outputs.append(mixture)
    difference = outputs[0] - diff_lambda[None, :, None] * outputs[1]
    normed = (
        difference
        * lax.rsqrt(jnp.mean(difference * difference, axis=-1, keepdims=True) + 1e-05)
        * 0.8
    )
    return (normed.astype(jnp.bfloat16).reshape(row_count, head_count * value_width), page_pool)


def send_buffer(page_pool, cont_table, cont_len, migration, reach, capacity):
    mig_slot = migration[:, 0]
    mig_off = migration[:, 1]
    entry_count = migration.shape[0]
    entry_order = jnp.arange(entry_count, dtype=jnp.int32)
    earlier = (mig_off[None, :] == mig_off[:, None]) & (entry_order[None, :] < entry_order[:, None])
    slot_place = (mig_off - 1) * capacity + jnp.sum(earlier.astype(jnp.int32), axis=1)
    page_rows = page_pool[cont_table[mig_slot]]
    page_rows = page_rows.reshape(entry_count, -1, page_pool.shape[-1])
    live_mask = (
        jnp.arange(page_rows.shape[1], dtype=jnp.int32)[None, :] <= cont_len[mig_slot][:, None]
    )
    page_rows = jnp.where(live_mask[:, :, None], page_rows, jnp.zeros_like(page_rows))
    buffer = (
        jnp.zeros((reach * capacity,) + page_rows.shape[1:], page_rows.dtype)
        .at[slot_place]
        .set(page_rows)
    )
    return buffer.reshape(reach, capacity, page_rows.shape[1], page_rows.shape[2])


def finish_rows(resid_rows, projected, norm_gain):
    summed = resid_rows.astype(jnp.float32) + projected
    normed = (
        summed * lax.rsqrt(jnp.mean(summed * summed, axis=-1, keepdims=True) + 1e-05) * norm_gain
    )
    return (summed.astype(jnp.bfloat16), normed.astype(jnp.bfloat16))


def shards(
    hidden_in,
    query,
    new_kv,
    pool_cache,
    prompt_table,
    prompt_len,
    req_group,
    cont_table,
    cont_len,
    migration,
    diff_lambda,
    out_weight,
    norm_gain,
):
    attention, page_pool = head_attention(
        query,
        new_kv,
        pool_cache,
        prompt_table,
        prompt_len,
        req_group,
        cont_table,
        cont_len,
        diff_lambda,
    )
    outgoing = send_buffer(page_pool, cont_table, cont_len, migration, MIG_REACH, MIG_CAP)
    received = [shifted(outgoing[offset - 1], "req", offset) for offset in range(1, MIG_REACH + 1)]
    arrived = jnp.stack(received, axis=0)
    arrived = arrived.reshape(-1, arrived.shape[2], arrived.shape[3])
    projected = jnp.dot(attention, out_weight, preferred_element_type=jnp.float32)
    total_sum = lax.psum(projected.astype(jnp.bfloat16), "tp").astype(jnp.float32)
    hidden_out, normed_out = finish_rows(hidden_in, total_sum, norm_gain)
    return (hidden_out, normed_out, arrived)


def solution(mesh):
    placed = (
        P("req", None),
        P("req", "tp"),
        P("req", "tp"),
        P("req", None, "tp"),
        P("req", None),
        P("req"),
        P("req"),
        P("req", None),
        P("req"),
        P("req", None),
        P("tp"),
        P("tp", None),
        P(),
    )
    return jax.shard_map(
        shards,
        mesh=mesh,
        in_specs=placed,
        out_specs=(P("req", None), P("req", None), P("req", None, "tp")),
        check_vma=False,
    )
```

profile of v0, /device:TPU:1, one launch (start us, length us, event | category | flops | bytes accessed | tf_op | source)
XLA Modules:
  0.0 116.2 jit_solution(18153596498102249846)
XLA Ops:
  7.3 3.6 %copy.59 = bf16[80,32,512]{2,1,0:T(8,128)(2,1)} copy(bf16[80,32,512]{2,1,0:T(8,128)(2,1)} %param.16) | data formatting | bytes 5242880
  11.0 0.7 gather_fusion.5
  12.0 2.6 %scatter_fusion = bf16[80,32,512]{2,1,0:T(8,128)(2,1)} fusion(bf16[80,32,512]{2,1,0:T(8,128)(2,1)} %copy.59, s32[16]{0:T(128)S(1)} %fusion.39, bf16[16,512]{1,0:T(8,128)(2,1)S(1)} %copy-done.5), kind=kCustom, calls=%fused_computation.6 | custom fusion | bytes 49280 | tf_op jit(solution)/shard_map/scatter | solution.py:35
  14.6 2.4 %gather_fusion.1 = bf16[32,32,512]{2,1,0:T(8,128)(2,1)S(1)} fusion(bf16[80,32,512]{2,1,0:T(8,128)(2,1)} %scatter_fusion, s32[1024]{0:T(1024)S(1)} %pad_clamp_fusion.2), kind=kCustom, calls=%fused_computation.1 | custom fusion | bytes 2097280 | tf_op jit(solution)/shard_map/gather | solution.py:37
  16.9 0.2 fusion.11
  17.2 0.2 fusion.10
  17.5 3.6 %gather_fusion = bf16[48,32,512]{2,1,0:T(8,128)(2,1)} fusion(bf16[80,32,512]{2,1,0:T(8,128)(2,1)} %scatter_fusion, s32[1024]{0:T(1024)S(1)} %pad_clamp_fusion.3), kind=kCustom, calls=%fused_computation | custom fusion | bytes 3145920 | tf_op jit(solution)/shard_map/gather | solution.py:36
  21.2 1.4 %fusion.44 = (f32[16]{0:T(128)S(1)}, f32[16,1,2,768]{3,0,2,1:T(8,128)S(1)}) fusion(bf16[16,128,1]{1,0,2:T(8,128)(2,1)S(1)} %get-tuple-element.25, bf16[2,768,1,512]{3,1,0,2:T(8,128)(2,1)} %bitcast.138, pred[2,768]{1,0:T(4,128)(4,1)S(1)} %iota_compare_fusion.1, pred[16,2]{0,1:T(4,128)(4,1)S(1)} %iota_compare_fusion.4), kind=kOutput, calls=%fused_computation.114 | convolution fusion | flops 6389744 | bytes 497248 | tf_op jit(solution)/shard_map/rhd,gjhd->rhgj/dot_general | solution.py:54
  22.7 1.3 %fusion.43 = (f32[16]{0:T(128)S(1)}, f32[16,1,2,768]{3,0,2,1:T(8,128)S(1)}) fusion(bf16[16,128,1]{1,0,2:T(8,128)(2,1)S(1)} %get-tuple-element.26, bf16[2,768,1,512]{3,1,0,2:T(8,128)(2,1)} %bitcast.139, pred[2,768]{1,0:T(4,128)(4,1)S(1)} %iota_compare_fusion.1, pred[16,2]{0,1:T(4,128)(4,1)S(1)} %iota_compare_fusion.4), kind=kOutput, calls=%fused_computation.113 | convolution fusion | flops 6389744 | bytes 497248 | tf_op jit(solution)/shard_map/rhd,gjhd->rhgj/dot_general | solution.py:54
  24.0 0.2 fusion.30
  24.2 0.2 fusion.28
  24.4 0.2 fusion.14
  24.6 0.2 fusion.13
  24.9 0.2 fusion.8
  25.1 0.2 fusion.9
  25.3 0.3 fusion.7
  26.2 0.4 multiply_reduce_fusion.1
  26.6 0.9 convolution_convert_fusion
  27.7 0.6 gather_fusion.2
  28.3 0.6 gather_fusion.3
  29.2 2.3 %gather_fusion.4 = bf16[12,32,512]{2,1,0:T(8,128)(2,1)S(1)} fusion(bf16[80,32,512]{2,1,0:T(8,128)(2,1)} %scatter_fusion, s32[1024]{0:T(1024)S(1)} %pad_clamp_fusion), kind=kCustom, calls=%fused_computation.4 | custom fusion | bytes 786480 | tf_op jit(solution)/shard_map/gather | solution.py:102
  31.5 0.2 convert_reduce_fusion
  31.7 0.1 bitcast_select_fusion
  31.9 0.8 scatter_fusion.1
  32.8 4.0 %collective-permute-start = (bf16[2,64,512]{2,1,0:T(8,128)(2,1)S(1)}, bf16[2,64,512]{2,1,0:T(8,128)(2,1)S(1)}, u32[]{:S(2)}, u32[]{:S(2)}) collective-permute-start(bf16[2,64,512]{2,1,0:T(8,128)(2,1)S(1)} %get-tuple-element.7), channel_id=1, source_target_pairs={{0,8},{8,16},{16,24},{24,32},{32,40},{40,48},{48,56},{56,64},{64,7... | collective-permute-start | bytes 393224 | tf_op jit(solution)/shard_map/ppermute | solution.py:13
  36.9 4.5 %collective-permute-start.1 = (bf16[2,64,512]{2,1,0:T(8,128)(2,1)S(1)}, bf16[2,64,512]{2,1,0:T(8,128)(2,1)S(1)}, u32[]{:S(2)}, u32[]{:S(2)}) collective-permute-start(bf16[2,64,512]{2,1,0:T(8,128)(2,1)S(1)} %get-tuple-element.10), channel_id=1, source_target_pairs={{0,16},{8,24},{16,32},{24,40},{32,48},{40,56},{48,64},{56,72},{64,... | collective-permute-start | bytes 393224 | tf_op jit(solution)/shard_map/ppermute | solution.py:13
  41.4 4.3 %collective-permute-start.2 = (bf16[2,64,512]{2,1,0:T(8,128)(2,1)S(1)}, bf16[2,64,512]{2,1,0:T(8,128)(2,1)S(1)}, u32[]{:S(2)}, u32[]{:S(2)}) collective-permute-start(bf16[2,64,512]{2,1,0:T(8,128)(2,1)S(1)} %get-tuple-element.9), channel_id=1, source_target_pairs={{0,24},{8,32},{16,40},{24,48},{32,56},{40,64},{48,72},{56,80},{64,... | collective-permute-start | bytes 393224 | tf_op jit(solution)/shard_map/ppermute | solution.py:13
  45.7 3.5 %collective-permute-start.3 = (bf16[2,64,512]{2,1,0:T(8,128)(2,1)S(1)}, bf16[2,64,512]{2,1,0:T(8,128)(2,1)S(1)}, u32[]{:S(2)}, u32[]{:S(2)}) collective-permute-start(bf16[2,64,512]{2,1,0:T(8,128)(2,1)S(1)} %get-tuple-element.8), channel_id=1, source_target_pairs={{0,32},{8,40},{16,48},{24,56},{32,64},{40,72},{48,80},{56,88},{64,... | collective-permute-start | bytes 393224 | tf_op jit(solution)/shard_map/ppermute | solution.py:13
  49.3 56.6 %all-reduce.2.cloned.1.call-done = bf16[16,2048]{1,0:T(8,128)(2,1)} async-done(((bf16[16,2048]{1,0:T(8,128)(2,1)}), bf16[16,2048]{1,0:T(8,128)(2,1)}) %all-reduce.2.cloned.1.call-update) | async-done | bytes 65552 | tf_op jit(solution)/shard_map/psum | solution.py:155
  105.9 1.0 multiply_reduce_fusion
  106.9 1.6 %multiply_convert_fusion = (bf16[16,2048]{1,0:T(8,128)(2,1)}, bf16[16,2048]{1,0:T(8,128)(2,1)}) fusion(bf16[16,2048]{1,0:T(8,128)(2,1)} %all-reduce.2.cloned.1.call-done, bf16[16,2048]{1,0:T(8,128)(2,1)S(1)} %copy-done.4, f32[2048]{0:T(1024)S(1)} %copy-done.6, f32[16]{0:T(128)S(1)} %add_rsqrt_fusion), kind=kLoop, calls=%fused_computation.33 | loop fusion | flops 229376 | bytes 270400 | tf_op jit(solution)/shard_map/convert_element_type | solution.py:121
  108.5 0.9 pad_maximum_fusion
  (66 shorter events, 1.2 us)
Async XLA Ops:
  7.2 19.4 %copy-start = (bf16[256,2048]{1,0:T(8,128)(2,1)S(1)}, bf16[256,2048]{1,0:T(8,128)(2,1)}, u32[]{:S(2)}) copy-start(bf16[256,2048]{1,0:T(8,128)(2,1)} %param.24) | copy-start | bytes 3145732
  7.2 4.7 %copy-start.7 = (bf16[16,256]{1,0:T(8,128)(2,1)S(1)}, bf16[16,256]{1,0:T(8,128)(2,1)}, u32[]{:S(2)}) copy-start(bf16[16,256]{1,0:T(8,128)(2,1)} %param.14) | copy-start | bytes 24580
  7.2 4.8 %copy-start.5 = (bf16[16,512]{1,0:T(8,128)(2,1)S(1)}, bf16[16,512]{1,0:T(8,128)(2,1)}, u32[]{:S(2)}) copy-start(bf16[16,512]{1,0:T(8,128)(2,1)} %param.15) | copy-start | bytes 49156
  7.2 3.8 %copy-start.2 = (s32[16,2]{0,1:T(2,128)S(1)}, s32[16,2]{0,1:T(2,128)}, u32[]{:S(2)}) copy-start(s32[16,2]{0,1:T(2,128)} %param.20) | copy-start | bytes 388
  7.2 3.7 %copy-start.1 = (s32[16]{0:T(128)S(1)}, s32[16]{0:T(128)}, u32[]{:S(2)}) copy-start(s32[16]{0:T(128)} %param.21) | copy-start | bytes 196
  7.2 98.7 %all-reduce.2.cloned.1.call-start = ((), (), s32[]{:S(2)}) async-start(), calls=%async_computation | async-start | bytes 131072 | tf_op jit(solution)/shard_map/psum | solution.py:155
  12.0 5.5 %copy-start.8 = (s32[2,24]{1,0:T(2,128)S(1)}, s32[2,24]{1,0:T(2,128)}, u32[]{:S(2)}) copy-start(s32[2,24]{1,0:T(2,128)} %param.17) | copy-start | bytes 580
  17.5 3.6 %copy-start.10 = (s32[2]{0:T(128)S(1)}, s32[2]{0:T(128)}, u32[]{:S(2)}) copy-start(s32[2]{0:T(128)} %param.18) | copy-start | bytes 28
  17.5 3.7 %copy-start.11 = (s32[16]{0:T(128)S(1)}, s32[16]{0:T(128)}, u32[]{:S(2)}) copy-start(s32[16]{0:T(128)} %param.19) | copy-start | bytes 196
  21.2 4.1 %copy-start.3 = (bf16[48,32,512]{2,1,0:T(8,128)(2,1)S(1)}, bf16[48,32,512]{2,1,0:T(8,128)(2,1)}, u32[]{:S(2)}) copy-start(bf16[48,32,512]{2,1,0:T(8,128)(2,1)} %gather_fusion) | copy-start | bytes 4718596
  25.3 2.4 %copy-start.9 = (s32[6,2]{0,1:T(2,128)S(1)}, s32[6,2]{0,1:T(2,128)}, u32[]{:S(2)}) copy-start(s32[6,2]{0,1:T(2,128)} %param.22) | copy-start | bytes 148
  31.9 74.1 %copy-start.4 = (bf16[16,2048]{1,0:T(8,128)(2,1)S(1)}, bf16[16,2048]{1,0:T(8,128)(2,1)}, u32[]{:S(2)}) copy-start(bf16[16,2048]{1,0:T(8,128)(2,1)} %param.13) | copy-start | bytes 196612
  31.9 75.0 %copy-start.6 = (f32[2048]{0:T(1024)S(1)}, f32[2048]{0:T(1024)}, u32[]{:S(2)}) copy-start(f32[2048]{0:T(1024)} %param.25) | copy-start | bytes 24580
  32.8 75.7 %collective-permute-start = (bf16[2,64,512]{2,1,0:T(8,128)(2,1)S(1)}, bf16[2,64,512]{2,1,0:T(8,128)(2,1)S(1)}, u32[]{:S(2)}, u32[]{:S(2)}) collective-permute-start(bf16[2,64,512]{2,1,0:T(8,128)(2,1)S(1)} %get-tuple-element.7), channel_id=1, source_target_pairs={{0,8},{8,16},{16,24},{24,32},{32,40},{40,48},{48,56},{56,64},{64,7... | collective-permute-start | bytes 393224 | tf_op jit(solution)/shard_map/ppermute | solution.py:13
  36.9 71.6 %collective-permute-start.1 = (bf16[2,64,512]{2,1,0:T(8,128)(2,1)S(1)}, bf16[2,64,512]{2,1,0:T(8,128)(2,1)S(1)}, u32[]{:S(2)}, u32[]{:S(2)}) collective-permute-start(bf16[2,64,512]{2,1,0:T(8,128)(2,1)S(1)} %get-tuple-element.10), channel_id=1, source_target_pairs={{0,16},{8,24},{16,32},{24,40},{32,48},{40,56},{48,64},{56,72},{64,... | collective-permute-start | bytes 393224 | tf_op jit(solution)/shard_map/ppermute | solution.py:13
  41.4 67.1 %collective-permute-start.2 = (bf16[2,64,512]{2,1,0:T(8,128)(2,1)S(1)}, bf16[2,64,512]{2,1,0:T(8,128)(2,1)S(1)}, u32[]{:S(2)}, u32[]{:S(2)}) collective-permute-start(bf16[2,64,512]{2,1,0:T(8,128)(2,1)S(1)} %get-tuple-element.9), channel_id=1, source_target_pairs={{0,24},{8,32},{16,40},{24,48},{32,56},{40,64},{48,72},{56,80},{64,... | collective-permute-start | bytes 393224 | tf_op jit(solution)/shard_map/ppermute | solution.py:13
  45.7 62.8 %collective-permute-start.3 = (bf16[2,64,512]{2,1,0:T(8,128)(2,1)S(1)}, bf16[2,64,512]{2,1,0:T(8,128)(2,1)S(1)}, u32[]{:S(2)}, u32[]{:S(2)}) collective-permute-start(bf16[2,64,512]{2,1,0:T(8,128)(2,1)S(1)} %get-tuple-element.8), channel_id=1, source_target_pairs={{0,32},{8,40},{16,48},{24,56},{32,64},{40,72},{48,80},{56,88},{64,... | collective-permute-start | bytes 393224 | tf_op jit(solution)/shard_map/ppermute | solution.py:13
Sparse Core Ops, SparseCore 0:
  27.7 78.2 all-reduce.1
where the time goes:
time: 117 us; the launch traced here: 116 us
  waiting for transfers between devices  56.7 us (48%)
  local copies, waits for them, and re-layouts  18 us (15%)
  starting transfers between devices  16.5 us (14%)
  between operations  15 us (13%)
  matrix products  5.16 us (4%)
  other arithmetic  4.85 us (4%)
    psum x1, waiting for transfers between devices, shards(): lax.psum(projected.astype(jnp.bfloat16), 'tp').astype(jnp.float32)  56.6 us
    ppermute x4, starting transfers between devices, shifted(): return lax.ppermute(value, axis, pairs)  16.4 us
    unnamed x27, local copies, waits for them, and re-layouts  3.8 us
    gather x1, local copies, waits for them, and re-layouts, head_attention(): page_pool[prompt_table].reshape(group_count, -1, head_count, head_width)  3.61 us
    gather x3, local copies, waits for them, and re-layouts, send_buffer(): page_rows = page_pool[cont_table[mig_slot]]  2.96 us
    dot_general x2, matrix products, head_attention(): jnp.einsum('rhd,gjhd->rhgj', split_query[:, :, twin_map], prompt_keys[......  2.75 us
    scatter x1, local copies, waits for them, and re-layouts, head_attention(): page_pool = page_pool.at[page_of, cont_len % page_len].set(new_rows)  2.59 us
    gather x1, local copies, waits for them, and re-layouts, head_attention(): page_pool[cont_table].reshape(row_count, -1, head_count, head_width)  2.35 us
  transfers between devices with their start and end apart: 5, of which 1 were waited for; matrix products, arithmetic and copies ran while one was open for 7% of the time, Pallas kernels for 0%

commit v1 on v0

v1 whole, which is shorter than its diff:
```python
import functools

import jax
import jax.numpy as jnp
from jax import lax
from jax.experimental import pallas as pl
from jax.experimental.pallas import tpu as pltpu
from jax.sharding import PartitionSpec as P

MIG_REACH = 4
MIG_CAP = 2
POOL_CHUNKS = 5
MESH = pl.DeviceIdType.MESH
F32 = jnp.float32
BF16 = jnp.bfloat16
NEG = -1e30


def layer_kernel(
    n_req,
    n_tp,
    prompt_table,
    prompt_len,
    req_group,
    cont_table,
    cont_len,
    migration,
    diff_lambda,
    hidden_in,
    query,
    new_kv,
    norm_gain,
    pool_hbm,
    weight_hbm,
    hidden_out,
    normed_out,
    arrived,
    pool,
    weight,
    new_rows,
    outgoing,
    part,
    sum_in,
    total,
    pool_sem,
    weight_sem,
    mig_send,
    mig_recv,
    sum_send,
    sum_recv,
    all_send,
    all_recv,
):
    rows, key_width = query.shape[0], query.shape[1] // 2
    pages, page_len, width = pool.shape
    value_col = 2 * key_width
    groups, group_pages = prompt_table.shape
    cont_pages = cont_table.shape[0]
    moves = migration.shape[1]
    block = total.shape[2]
    my_req = lax.axis_index("req")
    my_tp = lax.axis_index("tp")

    per_chunk = pages // POOL_CHUNKS
    pool_copies = []
    for chunk in range(POOL_CHUNKS):
        piece = pl.ds(chunk * per_chunk, per_chunk)
        pool_copies.append(
            pltpu.make_async_copy(pool_hbm.at[piece], pool.at[piece], pool_sem.at[chunk])
        )
        pool_copies[-1].start()
    weight_copy = pltpu.make_async_copy(weight_hbm, weight, weight_sem)
    weight_copy.start()

    barrier = pltpu.get_barrier_semaphore()
    for offset in range(1, MIG_REACH + 1):
        for other in (my_req + offset, my_req + n_req - offset):
            pl.semaphore_signal(
                barrier, inc=1, device_id={"req": lax.rem(other, n_req)}, device_id_type=MESH
            )
    for step in range(1, n_tp):
        pl.semaphore_signal(
            barrier, inc=1, device_id={"tp": lax.rem(my_tp + step, n_tp)}, device_id_type=MESH
        )

    new_rows[...] = new_kv[...].astype(F32)
    slot_of = []
    for move in range(moves):
        rank = jnp.int32(0)
        for earlier in range(move):
            rank = rank + (migration[1, earlier] == migration[1, move]).astype(jnp.int32)
        slot_of.append((migration[1, move] - 1) * MIG_CAP + rank)
    page_pos = lax.broadcasted_iota(jnp.int32, (page_len, width), 0)

    for copy in pool_copies:
        copy.wait()

    mig_copies = []
    for offset in range(1, MIG_REACH + 1):
        for place in range(MIG_CAP):
            slot = (offset - 1) * MIG_CAP + place
            request, present = jnp.int32(0), jnp.int32(0)
            for move in range(moves):
                here = slot_of[move] == slot
                request = jnp.where(here, migration[0, move], request)
                present = jnp.where(here, 1, present)
            length = jnp.where(present == 1, cont_len[request], -1)
            new_row = new_rows[pl.ds(request, 1), :]
            for page in range(cont_pages):
                held = pool[cont_table[page, request]].astype(F32)
                pos = page_pos + page * page_len
                kept = jnp.where(pos < length, held, 0.0)
                kept = jnp.where(pos == length, new_row, kept)
                outgoing[slot, page * page_len : (page + 1) * page_len, :] = kept.astype(BF16)
        span = pl.ds((offset - 1) * MIG_CAP, MIG_CAP)
        mig_copies.append(
            pltpu.make_async_remote_copy(
                src_ref=outgoing.at[span],
                dst_ref=arrived.at[span],
                send_sem=mig_send.at[offset - 1],
                recv_sem=mig_recv.at[offset - 1],
                device_id={"req": lax.rem(my_req + offset, n_req)},
                device_id_type=MESH,
            )
        )
    pl.semaphore_wait(barrier, 2 * MIG_REACH + n_tp - 1)
    for copy in reversed(mig_copies):
        copy.start()

    tile_pages = 8
    tile = tile_pages * page_len
    group_tiles = group_pages // tile_pages
    cont_rows = tile_pages // cont_pages
    row = lax.broadcasted_iota(jnp.int32, (rows, tile), 0)
    lane = lax.broadcasted_iota(jnp.int32, (rows, tile), 1)
    group_row = jnp.zeros((rows, tile), jnp.int32)
    length_row = jnp.zeros((rows, tile), jnp.int32)
    for request in range(rows):
        group_row = jnp.where(row == request, req_group[request], group_row)
        length_row = jnp.where(row == request, cont_len[request], length_row)

    tiles = []
    for group in range(groups):
        limit = jnp.where(group_row == group, prompt_len[group], 0)
        for part_of in range(group_tiles):
            names = [prompt_table[group, part_of * tile_pages + j] for j in range(tile_pages)]
            tiles.append((names, lane + part_of * tile < limit))
    cont_span = cont_pages * page_len
    for first in range(0, rows, cont_rows):
        names = [
            cont_table[j % cont_pages, first + j // cont_pages] for j in range(tile_pages)
        ]
        start = (row - first) * cont_span
        tiles.append((names, (lane >= start) & (lane < start + length_row)))

    scale = key_width ** (-0.5)
    queries = [query[:, twin * key_width : (twin + 1) * key_width] for twin in range(2)]
    contract_last = (((1,), (1,)), ((), ()))

    def scores(keys, mask, twin):
        product = lax.dot_general(
            queries[twin], keys, contract_last, preferred_element_type=F32
        )
        return jnp.where(mask, product * scale, NEG)

    score_tiles = []
    for names, mask in tiles:
        pair = []
        for twin in range(2):
            cols = slice(twin * key_width, (twin + 1) * key_width)
            keys = jnp.concatenate([pool[name, :, cols] for name in names], axis=0)
            pair.append(scores(keys, mask, twin))
        score_tiles.append(jnp.concatenate(pair, axis=0))
    own = lax.broadcasted_iota(jnp.int32, (rows, rows), 0) == lax.broadcasted_iota(
        jnp.int32, (rows, rows), 1
    )
    new_score = jnp.concatenate(
        [
            scores(new_kv[:, twin * key_width : (twin + 1) * key_width], own, twin)
            for twin in range(2)
        ],
        axis=0,
    )
    peak = functools.reduce(jnp.maximum, score_tiles)
    top = jnp.maximum(
        jnp.max(peak, axis=1, keepdims=True), jnp.max(new_score, axis=1, keepdims=True)
    )
    exp_tiles = [jnp.exp(score - top) for score in score_tiles]
    new_exp = jnp.exp(new_score - top)
    denominator = jnp.sum(sum(exp_tiles), axis=1, keepdims=True) + jnp.sum(
        new_exp, axis=1, keepdims=True
    )
    inverse = 1.0 / denominator
    mixture = jnp.dot(
        (new_exp * inverse).astype(BF16), new_kv[:, value_col:], preferred_element_type=F32
    )
    for (names, _), exp_tile in zip(tiles, exp_tiles):
        values = jnp.concatenate([pool[name, :, value_col:] for name in names], axis=0)
        mixture = mixture + jnp.dot(
            (exp_tile * inverse).astype(BF16), values, preferred_element_type=F32
        )
    difference = mixture[:rows] - diff_lambda[0] * mixture[rows:]
    square = jnp.mean(difference * difference, axis=1, keepdims=True)
    attention = (difference * lax.rsqrt(square + 1e-05) * 0.8).astype(BF16)

    weight_copy.wait()

    def columns(index):
        return pl.ds(pl.multiple_of(index * block, block), block)

    sum_copies = []
    for step in (4, 3, 5, 2, 6, 1, 7):
        peer = lax.rem(my_tp + step, n_tp)
        part[step] = jnp.dot(
            attention, weight[:, columns(peer)], preferred_element_type=F32
        ).astype(BF16)
        copy = pltpu.make_async_remote_copy(
            src_ref=part.at[step],
            dst_ref=sum_in.at[step],
            send_sem=sum_send.at[step],
            recv_sem=sum_recv.at[step],
            device_id={"tp": peer},
            device_id_type=MESH,
        )
        copy.start()
        sum_copies.append((step, copy))
    own_part = jnp.dot(
        attention, weight[:, columns(my_tp)], preferred_element_type=F32
    )
    summed = hidden_in[:, columns(my_tp)].astype(F32) + own_part
    for step, copy in reversed(sum_copies):
        copy.wait_recv()
        summed = summed + sum_in[step].astype(F32)
    total[my_tp] = summed.astype(BF16)
    all_copies = []
    for step in (4, 3, 5, 2, 6, 1, 7):
        peer = lax.rem(my_tp + step, n_tp)
        copy = pltpu.make_async_remote_copy(
            src_ref=total.at[my_tp],
            dst_ref=total.at[my_tp],
            send_sem=all_send.at[step],
            recv_sem=all_recv.at[step],
            device_id={"tp": peer},
            device_id_type=MESH,
        )
        copy.start()
        all_copies.append(copy)
    for copy in reversed(all_copies):
        copy.wait_recv()
    blocks = [total[index].astype(F32) for index in range(n_tp)]
    square_sum = functools.reduce(jnp.add, [value * value for value in blocks])
    mean = jnp.sum(square_sum, axis=1, keepdims=True) / (block * n_tp)
    factor = lax.rsqrt(mean + 1e-05)
    for index, value in enumerate(blocks):
        cols = slice(index * block, (index + 1) * block)
        hidden_out[:, cols] = value.astype(BF16)
        normed_out[:, cols] = (value * factor * norm_gain[:, cols]).astype(BF16)
    for _, copy in sum_copies:
        copy.wait_send()
    for copy in all_copies:
        copy.wait_send()
    for copy in mig_copies:
        copy.wait()


def shards(
    n_req,
    n_tp,
    hidden_in,
    query,
    new_kv,
    pool_cache,
    prompt_table,
    prompt_len,
    req_group,
    cont_table,
    cont_len,
    migration,
    diff_lambda,
    out_weight,
    norm_gain,
):
    rows, model = hidden_in.shape
    pages, page_len, width = pool_cache.shape
    span = cont_table.shape[1] * page_len
    slots = MIG_REACH * MIG_CAP
    block = model // n_tp
    smem = pl.BlockSpec(memory_space=pltpu.SMEM)
    vmem = pl.BlockSpec(memory_space=pltpu.VMEM)
    hbm = pl.BlockSpec(memory_space=pl.ANY)
    return pl.pallas_call(
        functools.partial(layer_kernel, n_req, n_tp),
        out_shape=(
            jax.ShapeDtypeStruct((rows, model), BF16),
            jax.ShapeDtypeStruct((rows, model), BF16),
            jax.ShapeDtypeStruct((slots, span, width), BF16),
        ),
        in_specs=[smem] * 7 + [vmem] * 4 + [hbm] * 2,
        out_specs=(vmem, vmem, vmem),
        scratch_shapes=[
            pltpu.VMEM((pages, page_len, width), BF16),
            pltpu.VMEM(out_weight.shape, BF16),
            pltpu.VMEM((rows, width), F32),
            pltpu.VMEM((slots, span, width), BF16),
            pltpu.VMEM((n_tp, rows, block), BF16),
            pltpu.VMEM((n_tp, rows, block), BF16),
            pltpu.VMEM((n_tp, rows, block), BF16),
            pltpu.SemaphoreType.DMA((POOL_CHUNKS,)),
            pltpu.SemaphoreType.DMA,
            pltpu.SemaphoreType.DMA((MIG_REACH,)),
            pltpu.SemaphoreType.DMA((MIG_REACH,)),
            pltpu.SemaphoreType.DMA((n_tp,)),
            pltpu.SemaphoreType.DMA((n_tp,)),
            pltpu.SemaphoreType.DMA((n_tp,)),
            pltpu.SemaphoreType.DMA((n_tp,)),
        ],
        compiler_params=pltpu.CompilerParams(collective_id=0, has_side_effects=True),
        name="decode_layer",
    )(
        prompt_table,
        prompt_len,
        req_group,
        cont_table.T,
        cont_len,
        migration.T,
        diff_lambda,
        hidden_in,
        query,
        new_kv,
        norm_gain.reshape(1, model),
        pool_cache,
        out_weight,
    )


def solution(mesh):
    placed = (
        P("req", None),
        P("req", "tp"),
        P("req", "tp"),
        P("req", None, "tp"),
        P("req", None),
        P("req"),
        P("req"),
        P("req", None),
        P("req"),
        P("req", None),
        P("tp"),
        P("tp", None),
        P(),
    )
    return jax.shard_map(
        functools.partial(shards, mesh.shape["req"], mesh.shape["tp"]),
        mesh=mesh,
        in_specs=placed,
        out_specs=(P("req", None), P("req", None), P("req", None, "tp")),
        check_vma=False,
    )
```

time: 117 us -> 37.2 us (0.32)
  waiting for transfers between devices: 56.7 us -> 0 us
  Pallas kernels: 0 us -> 30.8 us
  starting transfers between devices: 16.5 us -> 0 us
  between operations: 15 us -> 1.29 us
  local copies, waits for them, and re-layouts: 18 us -> 4.81 us
  matrix products: 5.16 us -> 0 us
  other arithmetic: 4.85 us -> 0 us
    psum x1 -> x0, waiting for transfers between devices: 56.6 us -> none  [shards(): lax.psum(projected.astype(jnp.bfloat16), 'tp').astype(jnp.float32)]
    pallas_call x0 -> x1, Pallas kernels: none -> 30.8 us  [shards(): pl.pallas_call(functools.partial(layer_kernel, n_req, n_tp), out_shape=(j...]
    ppermute x4 -> x0, starting transfers between devices: 16.4 us -> none  [shifted(): return lax.ppermute(value, axis, pairs)]
    gather x7 -> x0, local copies, waits for them, and re-layouts: 10.3 us -> none  [the longest x1 3.61 us: head_attention(): page_pool[prompt_table].reshape(group_count, -1, head_count, head_width)]
    dot_general x9 -> x0, matrix products: 5.16 us -> none  [the longest x2 2.75 us: head_attention(): jnp.einsum('rhd,gjhd->rhgj', split_query[:, :, twin_map], prompt_keys[......]
    scatter x2 -> x0, local copies, waits for them, and re-layouts: 3.41 us -> none  [the longest x1 2.59 us: head_attention(): page_pool = page_pool.at[page_of, cont_len % page_len].set(new_rows)]
    reduce_sum x5 -> x0, other arithmetic: 1.75 us -> none  [the longest x1 0.97 us: finish_rows(): jnp.mean(summed * summed, axis=-1, keepdims=True) + 1e-05]
    convert_element_type x2 -> x0, other arithmetic: 1.64 us -> none  [the longest x1 1.56 us: finish_rows(): return (summed.astype(jnp.bfloat16), normed.astype(jnp.bfloat16))]
  transfers between devices with their start and end apart: 5 -> 0, of which waited for: 1 -> 0; matrix products, arithmetic and copies ran while one was open for 7% -> 0% of each run, Pallas kernels for 0% -> 0%
where the time goes in v1:
time: 37.2 us; the launch traced here: 36.9 us
  Pallas kernels  30.8 us (83%)
  local copies, waits for them, and re-layouts  4.81 us (13%)
  between operations  1.29 us (3%)
    pallas_call x1, Pallas kernels, shards(): pl.pallas_call(functools.partial(layer_kernel, n_req, n_tp), out_shape=(j...  30.8 us
    unnamed x3, local copies, waits for them, and re-layouts  4.81 us

profile of v1, /device:TPU:1, one launch (start us, length us, event | category | flops | bytes accessed | tf_op | source)
XLA Modules:
  0.0 36.9 jit_solution(12408885848617678457)
XLA Ops:
  1.3 30.8 %decode_layer.1 = (bf16[16,2048]{1,0:T(8,128)(2,1)}, bf16[16,2048]{1,0:T(8,128)(2,1)}, bf16[8,64,512]{2,1,0:T(8,128)(2,1)}) custom-call(s32[2,24]{1,0:T(2,128)} %prompt_table.1, s32[2]{0:T(128)} %prompt_len.1, s32[16]{0:T(128)} %req_group.1, s32[2,16]{1,0:T(2,128)} %bitcast.4, s32[16]{0:T(128)} %cont_len.1, s32[2,6]{1,0:T(2,128)} %bitcast.5, ...), custom_call_target="tpu_custom_call" | custom-call | tf_op jit(solution)/shard_map/decode_layer/pallas_call | solution.py:291
  32.0 1.5 %copy.20 = bf16[16,2048]{1,0:T(8,128)(2,1)} copy(bf16[16,2048]{1,0:T(8,128)(2,1)} %get-tuple-element.6) | data formatting | bytes 131072
  33.5 1.5 %copy.21 = bf16[16,2048]{1,0:T(8,128)(2,1)} copy(bf16[16,2048]{1,0:T(8,128)(2,1)} %get-tuple-element.7) | data formatting | bytes 131072
  35.0 1.9 %copy.22 = bf16[8,64,512]{2,1,0:T(8,128)(2,1)} copy(bf16[8,64,512]{2,1,0:T(8,128)(2,1)} %get-tuple-element.8) | data formatting | bytes 1048576

commit v2 on v1

--- a/solution.py
+++ b/solution.py
@@ -19,6 +19,22 @@
 def layer_kernel(
     n_req,
     n_tp,
+    prompt_table_hbm,
+    prompt_len_hbm,
+    req_group_hbm,
+    cont_table_hbm,
+    cont_len_hbm,
+    migration_hbm,
+    diff_lambda_hbm,
+    hidden_in_hbm,
+    query_hbm,
+    new_kv_hbm,
+    norm_gain_hbm,
+    pool_hbm,
+    weight_hbm,
+    hidden_out,
+    normed_out,
+    arrived,
     prompt_table,
     prompt_len,
     req_group,
@@ -30,11 +46,6 @@
     query,
     new_kv,
     norm_gain,
-    pool_hbm,
-    weight_hbm,
-    hidden_out,
-    normed_out,
-    arrived,
     pool,
     weight,
     new_rows,
@@ -42,6 +53,7 @@
     part,
     sum_in,
     total,
+    small_sem,
     pool_sem,
     weight_sem,
     mig_send,
@@ -61,6 +73,25 @@
     my_req = lax.axis_index("req")
     my_tp = lax.axis_index("tp")
 
+    tables = (
+        (migration_hbm, migration),
+        (cont_table_hbm, cont_table),
+        (cont_len_hbm, cont_len),
+        (new_kv_hbm, new_kv),
+        (prompt_table_hbm, prompt_table),
+        (prompt_len_hbm, prompt_len),
+        (req_group_hbm, req_group),
+        (diff_lambda_hbm, diff_lambda),
+        (query_hbm, query),
+        (hidden_in_hbm, hidden_in),
+        (norm_gain_hbm, norm_gain),
+    )
+    small_copies = [
+        pltpu.make_async_copy(source, target, small_sem.at[index])
+        for index, (source, target) in enumerate(tables)
+    ]
+    for copy in small_copies[:4]:
+        copy.start()
     per_chunk = pages // POOL_CHUNKS
     pool_copies = []
     for chunk in range(POOL_CHUNKS):
@@ -70,6 +101,8 @@
         )
         pool_copies[-1].start()
     weight_copy = pltpu.make_async_copy(weight_hbm, weight, weight_sem)
+    for copy in small_copies[4:]:
+        copy.start()
     weight_copy.start()
 
     barrier = pltpu.get_barrier_semaphore()
@@ -83,6 +116,8 @@
             barrier, inc=1, device_id={"tp": lax.rem(my_tp + step, n_tp)}, device_id_type=MESH
         )
 
+    for copy in small_copies[:4]:
+        copy.wait()
     new_rows[...] = new_kv[...].astype(F32)
     slot_of = []
     for move in range(moves):
@@ -127,6 +162,8 @@
     for copy in reversed(mig_copies):
         copy.start()
 
+    for copy in small_copies[4:]:
+        copy.wait()
     tile_pages = 8
     tile = tile_pages * page_len
     group_tiles = group_pages // tile_pages
@@ -260,6 +297,18 @@
     for copy in all_copies:
         copy.wait_send()
     for copy in mig_copies:
+        copy.wait()
+
+
+def store_kernel(*refs):
+    count = len(refs) // 2
+    copies = [
+        pltpu.make_async_copy(refs[index], refs[count + index], refs[-1].at[index])
+        for index in range(count)
+    ]
+    for copy in copies:
+        copy.start()
+    for copy in copies:
         copy.wait()
 
 
@@ -285,38 +334,7 @@
     span = cont_table.shape[1] * page_len
     slots = MIG_REACH * MIG_CAP
     block = model // n_tp
-    smem = pl.BlockSpec(memory_space=pltpu.SMEM)
-    vmem = pl.BlockSpec(memory_space=pltpu.VMEM)
-    hbm = pl.BlockSpec(memory_space=pl.ANY)
-    return pl.pallas_call(
-        functools.partial(layer_kernel, n_req, n_tp),
-        out_shape=(
-            jax.ShapeDtypeStruct((rows, model), BF16),
-            jax.ShapeDtypeStruct((rows, model), BF16),
-            jax.ShapeDtypeStruct((slots, span, width), BF16),
-        ),
-        in_specs=[smem] * 7 + [vmem] * 4 + [hbm] * 2,
-        out_specs=(vmem, vmem, vmem),
-        scratch_shapes=[
-            pltpu.VMEM((pages, page_len, width), BF16),
-            pltpu.VMEM(out_weight.shape, BF16),
-            pltpu.VMEM((rows, width), F32),
-            pltpu.VMEM((slots, span, width), BF16),
-            pltpu.VMEM((n_tp, rows, block), BF16),
-            pltpu.VMEM((n_tp, rows, block), BF16),
-            pltpu.VMEM((n_tp, rows, block), BF16),
-            pltpu.SemaphoreType.DMA((POOL_CHUNKS,)),
-            pltpu.SemaphoreType.DMA,
-            pltpu.SemaphoreType.DMA((MIG_REACH,)),
-            pltpu.SemaphoreType.DMA((MIG_REACH,)),
-            pltpu.SemaphoreType.DMA((n_tp,)),
-            pltpu.SemaphoreType.DMA((n_tp,)),
-            pltpu.SemaphoreType.DMA((n_tp,)),
-            pltpu.SemaphoreType.DMA((n_tp,)),
-        ],
-        compiler_params=pltpu.CompilerParams(collective_id=0, has_side_effects=True),
-        name="decode_layer",
-    )(
+    operands = (
         prompt_table,
         prompt_len,
         req_group,
@@ -331,6 +349,43 @@
         pool_cache,
         out_weight,
     )
+    anywhere = pl.BlockSpec(memory_space=pl.ANY)
+    vmem = pl.BlockSpec(memory_space=pltpu.VMEM)
+    shapes = ((rows, model), (rows, model), (slots, span, width))
+    results = pl.pallas_call(
+        functools.partial(layer_kernel, n_req, n_tp),
+        out_shape=tuple(pltpu.VMEM(shape, BF16) for shape in shapes),
+        in_specs=[anywhere] * len(operands),
+        out_specs=(vmem,) * len(shapes),
+        scratch_shapes=[
+            *(pltpu.SMEM(value.shape, value.dtype) for value in operands[:7]),
+            *(pltpu.VMEM(value.shape, value.dtype) for value in operands[7:]),
+            pltpu.VMEM((rows, width), F32),
+            pltpu.VMEM((slots, span, width), BF16),
+            pltpu.VMEM((n_tp, rows, block), BF16),
+            pltpu.VMEM((n_tp, rows, block), BF16),
+            pltpu.VMEM((n_tp, rows, block), BF16),
+            pltpu.SemaphoreType.DMA((11,)),
+            pltpu.SemaphoreType.DMA((POOL_CHUNKS,)),
+            pltpu.SemaphoreType.DMA,
+            pltpu.SemaphoreType.DMA((MIG_REACH,)),
+            pltpu.SemaphoreType.DMA((MIG_REACH,)),
+            pltpu.SemaphoreType.DMA((n_tp,)),
+            pltpu.SemaphoreType.DMA((n_tp,)),
+            pltpu.SemaphoreType.DMA((n_tp,)),
+            pltpu.SemaphoreType.DMA((n_tp,)),
+        ],
+        compiler_params=pltpu.CompilerParams(collective_id=0, has_side_effects=True),
+        name="decode_layer",
+    )(*operands)
+    return pl.pallas_call(
+        store_kernel,
+        out_shape=tuple(jax.ShapeDtypeStruct(shape, BF16) for shape in shapes),
+        in_specs=[vmem] * len(shapes),
+        out_specs=(anywhere,) * len(shapes),
+        scratch_shapes=[pltpu.SemaphoreType.DMA((len(shapes),))],
+        name="store_results",
+    )(*(pltpu.with_memory_space_constraint(value, pltpu.VMEM) for value in results))
 
 
 def solution(mesh):

time: 37.2 us -> 31.4 us (0.84)
  local copies, waits for them, and re-layouts: 4.81 us -> 0 us
  Pallas kernels: 30.8 us -> 30 us
    unnamed x3 -> x0, local copies, waits for them, and re-layouts: 4.81 us -> none
    pallas_call x1 -> x2, Pallas kernels: 30.8 us -> 30 us  [the longest x1 29.2 us: shards(): pl.pallas_call(functools.partial(layer_kernel, n_req, n_tp), out_shape=tu...]
where the time goes in v2:
time: 31.4 us; the launch traced here: 31.3 us
  Pallas kernels  30 us (96%)
  between operations  1.29 us (4%)
    pallas_call x1, Pallas kernels, shards(): pl.pallas_call(functools.partial(layer_kernel, n_req, n_tp), out_shape=tu...  29.2 us
    pallas_call x1, Pallas kernels, shards(): pl.pallas_call(store_kernel, out_shape=tuple((jax.ShapeDtypeStruct(shape,...  0.86 us

profile of v2, /device:TPU:1, one launch (start us, length us, event | category | flops | bytes accessed | tf_op | source)
XLA Modules:
  0.0 31.3 jit_solution(11231789610361067997)
XLA Ops:
  1.3 29.2 %decode_layer.1 = (bf16[16,2048]{1,0:T(8,128)(2,1)S(1)}, bf16[16,2048]{1,0:T(8,128)(2,1)S(1)}, bf16[8,64,512]{2,1,0:T(8,128)(2,1)S(1)}) custom-call(s32[2,24]{1,0:T(2,128)} %prompt_table_hbm.1, s32[2]{0:T(128)} %prompt_len_hbm.1, s32[16]{0:T(128)} %req_group_hbm.1, s32[2,16]{1,0:T(2,128)} %bitcast.4, s32[16]{0:T(128)} %cont_len_hbm.1, s32[2,6]{1,0:T(2,128)} %bitcast.5, ...), custom_call_target="tpu_custom_call" | custom-call | tf_op jit(solution)/shard_map/decode_layer/pallas_call | solution.py:355
  30.4 0.9 %store_results.1 = (bf16[16,2048]{1,0:T(8,128)(2,1)}, bf16[16,2048]{1,0:T(8,128)(2,1)}, bf16[8,64,512]{2,1,0:T(8,128)(2,1)}) custom-call(bf16[16,2048]{1,0:T(8,128)(2,1)S(1)} %get-tuple-element.6.refs_0_, bf16[16,2048]{1,0:T(8,128)(2,1)S(1)} %get-tuple-element.7.refs_1_, bf16[8,64,512]{2,1,0:T(8,128)(2,1)S(1)} %get-tuple-element.8.refs_2_), custom_call_target="tpu_custom_call" | custom-call | tf_op jit(solution)/shard_map/store_results/pallas_call | solution.py:381

commit v3 on v2

--- a/solution.py
+++ b/solution.py
@@ -9,6 +9,11 @@
 
 MIG_REACH = 4
 MIG_CAP = 2
+SLOTS = MIG_REACH * MIG_CAP
+RELAYS = MIG_CAP
+ORDER = (0, 1, 2, 4, 5, 3, 6, 7)
+ROW = 4
+CONT_PAGES = 2
 POOL_CHUNKS = 5
 MESH = pl.DeviceIdType.MESH
 F32 = jnp.float32
@@ -49,6 +54,7 @@
     pool,
     weight,
     new_rows,
+    mixed,
     outgoing,
     part,
     sum_in,
@@ -130,10 +136,13 @@
     for copy in pool_copies:
         copy.wait()
 
-    mig_copies = []
-    for offset in range(1, MIG_REACH + 1):
-        for place in range(MIG_CAP):
-            slot = (offset - 1) * MIG_CAP + place
+    my_y = lax.rem(my_req, ROW)
+    far = (my_y == ROW - 1).astype(jnp.int32)
+
+    def send_pages():
+        pl.semaphore_wait(barrier, 2 * MIG_REACH + n_tp - 1)
+        for slot in ORDER:
+            offset = slot // MIG_CAP + 1
             request, present = jnp.int32(0), jnp.int32(0)
             for move in range(moves):
                 here = slot_of[move] == slot
@@ -141,105 +150,136 @@
                 present = jnp.where(here, 1, present)
             length = jnp.where(present == 1, cont_len[request], -1)
             new_row = new_rows[pl.ds(request, 1), :]
+            relayed = far if offset == 1 else 0
+            target = lax.rem(my_req + n_req + offset - ROW * relayed, n_req)
+            place = slot + SLOTS * relayed
             for page in range(cont_pages):
                 held = pool[cont_table[page, request]].astype(F32)
                 pos = page_pos + page * page_len
                 kept = jnp.where(pos < length, held, 0.0)
                 kept = jnp.where(pos == length, new_row, kept)
-                outgoing[slot, page * page_len : (page + 1) * page_len, :] = kept.astype(BF16)
-        span = pl.ds((offset - 1) * MIG_CAP, MIG_CAP)
-        mig_copies.append(
-            pltpu.make_async_remote_copy(
-                src_ref=outgoing.at[span],
-                dst_ref=arrived.at[span],
-                send_sem=mig_send.at[offset - 1],
-                recv_sem=mig_recv.at[offset - 1],
-                device_id={"req": lax.rem(my_req + offset, n_req)},
-                device_id_type=MESH,
+                span = pl.ds(page * page_len, page_len)
+                outgoing[slot, span, :] = kept.astype(BF16)
+                pltpu.make_async_remote_copy(
+                    src_ref=outgoing.at[slot, span],
+                    dst_ref=arrived.at[place, span],
+                    send_sem=mig_send.at[slot],
+                    recv_sem=mig_recv.at[slot + relayed * (SLOTS + slot + page)],
+                    device_id={"req": target},
+                    device_id_type=MESH,
+                ).start()
+
+    def attend():
+        for copy in small_copies[4:]:
+            copy.wait()
+        tile_pages = 8
+        tile = tile_pages * page_len
+        group_tiles = group_pages // tile_pages
+        cont_rows = tile_pages // cont_pages
+        row = lax.broadcasted_iota(jnp.int32, (rows, tile), 0)
+        lane = lax.broadcasted_iota(jnp.int32, (rows, tile), 1)
+        group_row = jnp.zeros((rows, tile), jnp.int32)
+        length_row = jnp.zeros((rows, tile), jnp.int32)
+        for request in range(rows):
+            group_row = jnp.where(row == request, req_group[request], group_row)
+            length_row = jnp.where(row == request, cont_len[request], length_row)
+
+        tiles = []
+        for group in range(groups):
+            limit = jnp.where(group_row == group, prompt_len[group], 0)
+            for part_of in range(group_tiles):
+                names = [prompt_table[group, part_of * tile_pages + j] for j in range(tile_pages)]
+                tiles.append((names, lane + part_of * tile < limit))
+        cont_span = cont_pages * page_len
+        for first in range(0, rows, cont_rows):
+            names = [
+                cont_table[j % cont_pages, first + j // cont_pages] for j in range(tile_pages)
+            ]
+            start = (row - first) * cont_span
+            tiles.append((names, (lane >= start) & (lane < start + length_row)))
+
+        scale = key_width ** (-0.5)
+        queries = [query[:, twin * key_width : (twin + 1) * key_width] for twin in range(2)]
+        contract_last = (((1,), (1,)), ((), ()))
+
+        def scores(keys, mask, twin):
+            product = lax.dot_general(
+                queries[twin], keys, contract_last, preferred_element_type=F32
             )
-        )
-    pl.semaphore_wait(barrier, 2 * MIG_REACH + n_tp - 1)
-    for copy in reversed(mig_copies):
-        copy.start()
-
-    for copy in small_copies[4:]:
-        copy.wait()
-    tile_pages = 8
-    tile = tile_pages * page_len
-    group_tiles = group_pages // tile_pages
-    cont_rows = tile_pages // cont_pages
-    row = lax.broadcasted_iota(jnp.int32, (rows, tile), 0)
-    lane = lax.broadcasted_iota(jnp.int32, (rows, tile), 1)
-    group_row = jnp.zeros((rows, tile), jnp.int32)
-    length_row = jnp.zeros((rows, tile), jnp.int32)
-    for request in range(rows):
-        group_row = jnp.where(row == request, req_group[request], group_row)
-        length_row = jnp.where(row == request, cont_len[request], length_row)
-
-    tiles = []
-    for group in range(groups):
-        limit = jnp.where(group_row == group, prompt_len[group], 0)
-        for part_of in range(group_tiles):
-            names = [prompt_table[group, part_of * tile_pages + j] for j in range(tile_pages)]
-            tiles.append((names, lane + part_of * tile < limit))
-    cont_span = cont_pages * page_len
-    for first in range(0, rows, cont_rows):
-        names = [
-            cont_table[j % cont_pages, first + j // cont_pages] for j in range(tile_pages)
-        ]
-        start = (row - first) * cont_span
-        tiles.append((names, (lane >= start) & (lane < start + length_row)))
-
-    scale = key_width ** (-0.5)
-    queries = [query[:, twin * key_width : (twin + 1) * key_width] for twin in range(2)]
-    contract_last = (((1,), (1,)), ((), ()))
-
-    def scores(keys, mask, twin):
-        product = lax.dot_general(
-            queries[twin], keys, contract_last, preferred_element_type=F32
-        )
-        return jnp.where(mask, product * scale, NEG)
-
-    score_tiles = []
-    for names, mask in tiles:
-        pair = []
-        for twin in range(2):
-            cols = slice(twin * key_width, (twin + 1) * key_width)
-            keys = jnp.concatenate([pool[name, :, cols] for name in names], axis=0)
-            pair.append(scores(keys, mask, twin))
-        score_tiles.append(jnp.concatenate(pair, axis=0))
-    own = lax.broadcasted_iota(jnp.int32, (rows, rows), 0) == lax.broadcasted_iota(
-        jnp.int32, (rows, rows), 1
-    )
-    new_score = jnp.concatenate(
-        [
-            scores(new_kv[:, twin * key_width : (twin + 1) * key_width], own, twin)
-            for twin in range(2)
-        ],
-        axis=0,
-    )
-    peak = functools.reduce(jnp.maximum, score_tiles)
-    top = jnp.maximum(
-        jnp.max(peak, axis=1, keepdims=True), jnp.max(new_score, axis=1, keepdims=True)
-    )
-    exp_tiles = [jnp.exp(score - top) for score in score_tiles]
-    new_exp = jnp.exp(new_score - top)
-    denominator = jnp.sum(sum(exp_tiles), axis=1, keepdims=True) + jnp.sum(
-        new_exp, axis=1, keepdims=True
-    )
-    inverse = 1.0 / denominator
-    mixture = jnp.dot(
-        (new_exp * inverse).astype(BF16), new_kv[:, value_col:], preferred_element_type=F32
-    )
-    for (names, _), exp_tile in zip(tiles, exp_tiles):
-        values = jnp.concatenate([pool[name, :, value_col:] for name in names], axis=0)
-        mixture = mixture + jnp.dot(
-            (exp_tile * inverse).astype(BF16), values, preferred_element_type=F32
-        )
-    difference = mixture[:rows] - diff_lambda[0] * mixture[rows:]
-    square = jnp.mean(difference * difference, axis=1, keepdims=True)
-    attention = (difference * lax.rsqrt(square + 1e-05) * 0.8).astype(BF16)
-
+            return jnp.where(mask, product * scale, NEG)
+
+        score_tiles = []
+        for names, mask in tiles:
+            pair = []
+            for twin in range(2):
+                cols = slice(twin * key_width, (twin + 1) * key_width)
+                keys = jnp.concatenate([pool[name, :, cols] for name in names], axis=0)
+                pair.append(scores(keys, mask, twin))
+            score_tiles.append(jnp.concatenate(pair, axis=0))
+        own = lax.broadcasted_iota(jnp.int32, (rows, rows), 0) == lax.broadcasted_iota(
+            jnp.int32, (rows, rows), 1
+        )
+        new_score = jnp.concatenate(
+            [
+                scores(new_kv[:, twin * key_width : (twin + 1) * key_width], own, twin)
+                for twin in range(2)
+            ],
+            axis=0,
+        )
+        peak = functools.reduce(jnp.maximum, score_tiles)
+        top = jnp.maximum(
+            jnp.max(peak, axis=1, keepdims=True), jnp.max(new_score, axis=1, keepdims=True)
+        )
+        exp_tiles = [jnp.exp(score - top) for score in score_tiles]
+        new_exp = jnp.exp(new_score - top)
+        denominator = jnp.sum(sum(exp_tiles), axis=1, keepdims=True) + jnp.sum(
+            new_exp, axis=1, keepdims=True
+        )
+        inverse = 1.0 / denominator
+        mixture = jnp.dot(
+            (new_exp * inverse).astype(BF16), new_kv[:, value_col:], preferred_element_type=F32
+        )
+        for (names, _), exp_tile in zip(tiles, exp_tiles):
+            values = jnp.concatenate([pool[name, :, value_col:] for name in names], axis=0)
+            mixture = mixture + jnp.dot(
+                (exp_tile * inverse).astype(BF16), values, preferred_element_type=F32
+            )
+        difference = mixture[:rows] - diff_lambda[0] * mixture[rows:]
+        square = jnp.mean(difference * difference, axis=1, keepdims=True)
+        mixed[...] = (difference * lax.rsqrt(square + 1e-05) * 0.8).astype(BF16)
+
+
+    early = my_req < ROW
+
+    @pl.loop(0, 2)
+    def _(phase):
+        pl.when((phase == 0) == early)(attend)
+        pl.when((phase == 0) != early)(send_pages)
+
+    def relay(slot, page):
+        span = pl.ds(page * page_len, page_len)
+        return pltpu.make_async_remote_copy(
+            src_ref=arrived.at[SLOTS + slot, span],
+            dst_ref=arrived.at[slot, span],
+            send_sem=mig_send.at[SLOTS + slot],
+            recv_sem=mig_recv.at[slot],
+            device_id={"req": lax.rem(my_req + ROW, n_req)},
+            device_id_type=MESH,
+        )
+
+    def wait_bytes(ref, sem):
+        pltpu.make_async_copy(ref, ref, sem).wait()
+
+    def pass_on():
+        for slot in range(MIG_CAP):
+            for page in range(cont_pages):
+                span = pl.ds(page * page_len, page_len)
+                wait_bytes(
+                    arrived.at[SLOTS + slot, span], mig_recv.at[SLOTS + 2 * slot + page]
+                )
+                relay(slot, page).start()
+
+    attention = mixed[...]
     weight_copy.wait()
 
     def columns(index):
@@ -261,6 +301,7 @@
         )
         copy.start()
         sum_copies.append((step, copy))
+    pl.when(my_y == 0)(pass_on)
     own_part = jnp.dot(
         attention, weight[:, columns(my_tp)], preferred_element_type=F32
     )
@@ -296,14 +337,24 @@
         copy.wait_send()
     for copy in all_copies:
         copy.wait_send()
-    for copy in mig_copies:
-        copy.wait()
+    for slot in range(SLOTS):
+        wait_bytes(outgoing.at[slot], mig_send.at[slot])
+        wait_bytes(arrived.at[slot], mig_recv.at[slot])
+
+    @pl.when(my_y == 0)
+    def _():
+        for slot in range(MIG_CAP):
+            wait_bytes(arrived.at[SLOTS + slot], mig_send.at[SLOTS + slot])
 
 
 def store_kernel(*refs):
     count = len(refs) // 2
     copies = [
-        pltpu.make_async_copy(refs[index], refs[count + index], refs[-1].at[index])
+        pltpu.make_async_copy(
+            refs[index].at[pl.ds(0, refs[count + index].shape[0])],
+            refs[count + index],
+            refs[-1].at[index],
+        )
         for index in range(count)
     ]
     for copy in copies:
@@ -332,7 +383,6 @@
     rows, model = hidden_in.shape
     pages, page_len, width = pool_cache.shape
     span = cont_table.shape[1] * page_len
-    slots = MIG_REACH * MIG_CAP
     block = model // n_tp
     operands = (
         prompt_table,
@@ -351,25 +401,27 @@
     )
     anywhere = pl.BlockSpec(memory_space=pl.ANY)
     vmem = pl.BlockSpec(memory_space=pltpu.VMEM)
-    shapes = ((rows, model), (rows, model), (slots, span, width))
+    shapes = ((rows, model), (rows, model), (SLOTS, span, width))
+    landing = ((rows, model), (rows, model), (SLOTS + RELAYS, span, width))
     results = pl.pallas_call(
         functools.partial(layer_kernel, n_req, n_tp),
-        out_shape=tuple(pltpu.VMEM(shape, BF16) for shape in shapes),
+        out_shape=tuple(pltpu.VMEM(shape, BF16) for shape in landing),
         in_specs=[anywhere] * len(operands),
         out_specs=(vmem,) * len(shapes),
         scratch_shapes=[
             *(pltpu.SMEM(value.shape, value.dtype) for value in operands[:7]),
             *(pltpu.VMEM(value.shape, value.dtype) for value in operands[7:]),
             pltpu.VMEM((rows, width), F32),
-            pltpu.VMEM((slots, span, width), BF16),
+            pltpu.VMEM((rows, out_weight.shape[0]), BF16),
+            pltpu.VMEM((SLOTS, span, width), BF16),
             pltpu.VMEM((n_tp, rows, block), BF16),
             pltpu.VMEM((n_tp, rows, block), BF16),
             pltpu.VMEM((n_tp, rows, block), BF16),
             pltpu.SemaphoreType.DMA((11,)),
             pltpu.SemaphoreType.DMA((POOL_CHUNKS,)),
             pltpu.SemaphoreType.DMA,
-            pltpu.SemaphoreType.DMA((MIG_REACH,)),
-            pltpu.SemaphoreType.DMA((MIG_REACH,)),
+            pltpu.SemaphoreType.DMA((SLOTS + RELAYS,)),
+            pltpu.SemaphoreType.DMA((SLOTS + RELAYS * CONT_PAGES,)),
             pltpu.SemaphoreType.DMA((n_tp,)),
             pltpu.SemaphoreType.DMA((n_tp,)),
             pltpu.SemaphoreType.DMA((n_tp,)),

time: 31.4 us -> 27.1 us (0.86)
  Pallas kernels: 30 us -> 25.7 us
    pallas_call x1, Pallas kernels: 29.2 us -> 24.8 us  [shards(): pl.pallas_call(functools.partial(layer_kernel, n_req, n_tp), out_shape=tu...]
where the time goes in v3:
time: 27.1 us; the launch traced here: 27 us
  Pallas kernels  25.7 us (95%)
  between operations  1.29 us (5%)
    pallas_call x1, Pallas kernels, shards(): pl.pallas_call(functools.partial(layer_kernel, n_req, n_tp), out_shape=tu...  24.8 us
    pallas_call x1, Pallas kernels, shards(): pl.pallas_call(store_kernel, out_shape=tuple((jax.ShapeDtypeStruct(shape,...  0.86 us

profile of v3, /device:TPU:1, one launch (start us, length us, event | category | flops | bytes accessed | tf_op | source)
XLA Modules:
  0.0 27.0 jit_solution(10686557572391648751)
XLA Ops:
  1.3 24.8 %decode_layer.1 = (bf16[16,2048]{1,0:T(8,128)(2,1)S(1)}, bf16[16,2048]{1,0:T(8,128)(2,1)S(1)}, bf16[10,64,512]{2,1,0:T(8,128)(2,1)S(1)}) custom-call(s32[2,24]{1,0:T(2,128)} %prompt_table_hbm.1, s32[2]{0:T(128)} %prompt_len_hbm.1, s32[16]{0:T(128)} %req_group_hbm.1, s32[2,16]{1,0:T(2,128)} %bitcast.4, s32[16]{0:T(128)} %cont_len_hbm.1, s32[2,6]{1,0:T(2,128)} %bitcast.5, ...), custom_call_target="tpu_custom_call" | custom-call | tf_op jit(solution)/shard_map/decode_layer/pallas_call | solution.py:406
  26.1 0.9 %store_results.1 = (bf16[16,2048]{1,0:T(8,128)(2,1)}, bf16[16,2048]{1,0:T(8,128)(2,1)}, bf16[8,64,512]{2,1,0:T(8,128)(2,1)}) custom-call(bf16[16,2048]{1,0:T(8,128)(2,1)S(1)} %get-tuple-element.6.refs_0_, bf16[16,2048]{1,0:T(8,128)(2,1)S(1)} %get-tuple-element.7.refs_1_, bf16[10,64,512]{2,1,0:T(8,128)(2,1)S(1)} %get-tuple-element.8.refs_2_), custom_call_target="tpu_custom_call" | custom-call | tf_op jit(solution)/shard_map/store_results/pallas_call | solution.py:433

commit v4 on v3

--- a/solution.py
+++ b/solution.py
@@ -11,7 +11,6 @@
 MIG_CAP = 2
 SLOTS = MIG_REACH * MIG_CAP
 RELAYS = MIG_CAP
-ORDER = (0, 1, 2, 4, 5, 3, 6, 7)
 ROW = 4
 CONT_PAGES = 2
 POOL_CHUNKS = 5
@@ -109,14 +108,18 @@
     weight_copy = pltpu.make_async_copy(weight_hbm, weight, weight_sem)
     for copy in small_copies[4:]:
         copy.start()
-    weight_copy.start()
 
     barrier = pltpu.get_barrier_semaphore()
+    my_y = lax.rem(my_req, ROW)
+    far = (my_y == ROW - 1).astype(jnp.int32)
+    near = (my_y == 1).astype(jnp.int32)
     for offset in range(1, MIG_REACH + 1):
-        for other in (my_req + offset, my_req + n_req - offset):
-            pl.semaphore_signal(
-                barrier, inc=1, device_id={"req": lax.rem(other, n_req)}, device_id_type=MESH
-            )
+        source = my_req + n_req - offset
+        if offset == 2:
+            source = source + ROW * near
+        pl.semaphore_signal(
+            barrier, inc=1, device_id={"req": lax.rem(source, n_req)}, device_id_type=MESH
+        )
     for step in range(1, n_tp):
         pl.semaphore_signal(
             barrier, inc=1, device_id={"tp": lax.rem(my_tp + step, n_tp)}, device_id_type=MESH
@@ -135,14 +138,14 @@
 
     for copy in pool_copies:
         copy.wait()
-
-    my_y = lax.rem(my_req, ROW)
-    far = (my_y == ROW - 1).astype(jnp.int32)
+    weight_copy.start()
 
     def send_pages():
-        pl.semaphore_wait(barrier, 2 * MIG_REACH + n_tp - 1)
-        for slot in ORDER:
-            offset = slot // MIG_CAP + 1
+        pl.semaphore_wait(barrier, MIG_REACH + n_tp - 1)
+        first = MIG_CAP * (ROW - 1 - my_y)
+        for turn in range(SLOTS):
+            slot = lax.rem(first + turn, SLOTS)
+            offset = lax.div(slot, MIG_CAP) + 1
             request, present = jnp.int32(0), jnp.int32(0)
             for move in range(moves):
                 here = slot_of[move] == slot
@@ -150,9 +153,9 @@
                 present = jnp.where(here, 1, present)
             length = jnp.where(present == 1, cont_len[request], -1)
             new_row = new_rows[pl.ds(request, 1), :]
-            relayed = far if offset == 1 else 0
+            relayed = far if turn // MIG_CAP == 1 else 0
             target = lax.rem(my_req + n_req + offset - ROW * relayed, n_req)
-            place = slot + SLOTS * relayed
+            place = slot + (SLOTS - MIG_CAP) * relayed
             for page in range(cont_pages):
                 held = pool[cont_table[page, request]].astype(F32)
                 pos = page_pos + page * page_len
@@ -164,7 +167,7 @@
                     src_ref=outgoing.at[slot, span],
                     dst_ref=arrived.at[place, span],
                     send_sem=mig_send.at[slot],
-                    recv_sem=mig_recv.at[slot + relayed * (SLOTS + slot + page)],
+                    recv_sem=mig_recv.at[slot + relayed * (SLOTS - 2 * MIG_CAP + slot + page)],
                     device_id={"req": target},
                     device_id_type=MESH,
                 ).start()
@@ -249,20 +252,16 @@
         mixed[...] = (difference * lax.rsqrt(square + 1e-05) * 0.8).astype(BF16)
 
 
-    early = my_req < ROW
-
-    @pl.loop(0, 2)
-    def _(phase):
-        pl.when((phase == 0) == early)(attend)
-        pl.when((phase == 0) != early)(send_pages)
+    send_pages()
+    attend()
 
     def relay(slot, page):
         span = pl.ds(page * page_len, page_len)
         return pltpu.make_async_remote_copy(
             src_ref=arrived.at[SLOTS + slot, span],
-            dst_ref=arrived.at[slot, span],
+            dst_ref=arrived.at[MIG_CAP + slot, span],
             send_sem=mig_send.at[SLOTS + slot],
-            recv_sem=mig_recv.at[slot],
+            recv_sem=mig_recv.at[MIG_CAP + slot],
             device_id={"req": lax.rem(my_req + ROW, n_req)},
             device_id_type=MESH,
         )
@@ -301,7 +300,7 @@
         )
         copy.start()
         sum_copies.append((step, copy))
-    pl.when(my_y == 0)(pass_on)
+    pl.when(my_y == 1)(pass_on)
     own_part = jnp.dot(
         attention, weight[:, columns(my_tp)], preferred_element_type=F32
     )
@@ -341,7 +340,7 @@
         wait_bytes(outgoing.at[slot], mig_send.at[slot])
         wait_bytes(arrived.at[slot], mig_recv.at[slot])
 
-    @pl.when(my_y == 0)
+    @pl.when(my_y == 1)
     def _():
         for slot in range(MIG_CAP):
             wait_bytes(arrived.at[SLOTS + slot], mig_send.at[SLOTS + slot])

time: 27.1 us -> 25.7 us (0.948)
  Pallas kernels: 25.7 us -> 24.2 us
    pallas_call x1, Pallas kernels: 24.8 us -> 23.3 us  [shards(): pl.pallas_call(functools.partial(layer_kernel, n_req, n_tp), out_shape=tu...]
where the time goes in v4:
time: 25.7 us; the launch traced here: 25.5 us
  Pallas kernels  24.2 us (94%)
  between operations  1.29 us (5%)
    pallas_call x1, Pallas kernels, shards(): pl.pallas_call(functools.partial(layer_kernel, n_req, n_tp), out_shape=tu...  23.3 us
    pallas_call x1, Pallas kernels, shards(): pl.pallas_call(store_kernel, out_shape=tuple((jax.ShapeDtypeStruct(shape,...  0.86 us

profile of v4, /device:TPU:1, one launch (start us, length us, event | category | flops | bytes accessed | tf_op | source)
XLA Modules:
  0.0 25.5 jit_solution(3385633871047338398)
XLA Ops:
  1.3 23.3 %decode_layer.1 = (bf16[16,2048]{1,0:T(8,128)(2,1)S(1)}, bf16[16,2048]{1,0:T(8,128)(2,1)S(1)}, bf16[10,64,512]{2,1,0:T(8,128)(2,1)S(1)}) custom-call(s32[2,24]{1,0:T(2,128)} %prompt_table_hbm.1, s32[2]{0:T(128)} %prompt_len_hbm.1, s32[16]{0:T(128)} %req_group_hbm.1, s32[2,16]{1,0:T(2,128)} %bitcast.4, s32[16]{0:T(128)} %cont_len_hbm.1, s32[2,6]{1,0:T(2,128)} %bitcast.5, ...), custom_call_target="tpu_custom_call" | custom-call | tf_op jit(solution)/shard_map/decode_layer/pallas_call | solution.py:405
  24.6 0.9 %store_results.1 = (bf16[16,2048]{1,0:T(8,128)(2,1)}, bf16[16,2048]{1,0:T(8,128)(2,1)}, bf16[8,64,512]{2,1,0:T(8,128)(2,1)}) custom-call(bf16[16,2048]{1,0:T(8,128)(2,1)S(1)} %get-tuple-element.6.refs_0_, bf16[16,2048]{1,0:T(8,128)(2,1)S(1)} %get-tuple-element.7.refs_1_, bf16[10,64,512]{2,1,0:T(8,128)(2,1)S(1)} %get-tuple-element.8.refs_2_), custom_call_target="tpu_custom_call" | custom-call | tf_op jit(solution)/shard_map/store_results/pallas_call | solution.py:432

commit v5 on v4

--- a/solution.py
+++ b/solution.py
@@ -58,6 +58,7 @@
     part,
     sum_in,
     total,
+    ready,
     small_sem,
     pool_sem,
     weight_sem,
@@ -112,18 +113,27 @@
     barrier = pltpu.get_barrier_semaphore()
     my_y = lax.rem(my_req, ROW)
     far = (my_y == ROW - 1).astype(jnp.int32)
-    near = (my_y == 1).astype(jnp.int32)
+
+    def tell(semaphore, axis, index):
+        pl.semaphore_signal(
+            semaphore, inc=1, device_id={axis: index}, device_id_type=MESH
+        )
+
+    def req_at(step):
+        return lax.rem(my_req + n_req + step, n_req)
+
+    def tp_at(step):
+        return lax.rem(my_tp + n_tp + step, n_tp)
+
     for offset in range(1, MIG_REACH + 1):
-        source = my_req + n_req - offset
+        crosses = my_y < offset
         if offset == 2:
-            source = source + ROW * near
-        pl.semaphore_signal(
-            barrier, inc=1, device_id={"req": lax.rem(source, n_req)}, device_id_type=MESH
-        )
+            crosses = crosses & (my_y != 1)
+        pl.when(crosses)(functools.partial(tell, barrier, "req", req_at(-offset)))
+    for step in range(1, ROW):
+        pl.when(my_y + step < ROW)(functools.partial(tell, barrier, "req", req_at(step)))
     for step in range(1, n_tp):
-        pl.semaphore_signal(
-            barrier, inc=1, device_id={"tp": lax.rem(my_tp + step, n_tp)}, device_id_type=MESH
-        )
+        pl.when(my_tp + step < n_tp)(functools.partial(tell, barrier, "tp", tp_at(step)))
 
     for copy in small_copies[:4]:
         copy.wait()
@@ -141,9 +151,22 @@
     weight_copy.start()
 
     def send_pages():
-        pl.semaphore_wait(barrier, MIG_REACH + n_tp - 1)
+        pl.semaphore_wait(barrier, 2 * my_y + 1 - far + my_tp)
+        for step in range(1, ROW):
+            pl.when(my_y >= step)(
+                functools.partial(tell, ready.at[0], "req", req_at(-step))
+            )
+        for step in range(1, n_tp):
+            pl.when(my_tp >= step)(
+                functools.partial(tell, ready.at[1], "tp", tp_at(-step))
+            )
         first = MIG_CAP * (ROW - 1 - my_y)
         for turn in range(SLOTS):
+            if turn in range(MIG_CAP, SLOTS, MIG_CAP):
+                inner = turn // MIG_CAP - 1
+                pl.when(my_y == inner)(
+                    functools.partial(pl.semaphore_wait, ready.at[0], ROW - 1 - inner)
+                )
             slot = lax.rem(first + turn, SLOTS)
             offset = lax.div(slot, MIG_CAP) + 1
             request, present = jnp.int32(0), jnp.int32(0)
@@ -283,6 +306,11 @@
 
     def columns(index):
         return pl.ds(pl.multiple_of(index * block, block), block)
+
+
+    @pl.when(my_tp < n_tp - 1)
+    def _():
+        pl.semaphore_wait(ready.at[1], n_tp - 1 - my_tp)
 
     sum_copies = []
     for step in (4, 3, 5, 2, 6, 1, 7):
@@ -416,6 +444,7 @@
             pltpu.VMEM((n_tp, rows, block), BF16),
             pltpu.VMEM((n_tp, rows, block), BF16),
             pltpu.VMEM((n_tp, rows, block), BF16),
+            pltpu.SemaphoreType.REGULAR((2,)),
             pltpu.SemaphoreType.DMA((11,)),
             pltpu.SemaphoreType.DMA((POOL_CHUNKS,)),
             pltpu.SemaphoreType.DMA,

time: 25.7 us -> 24.1 us (0.938)
  the two profiles are of different devices: /device:TPU:1 before, /device:TPU:14 now
where the time goes in v5:
time: 24.1 us; the launch traced here: 23.9 us
  Pallas kernels  22.7 us (94%)
  between operations  1.29 us (5%)
    pallas_call x1, Pallas kernels, shards(): pl.pallas_call(functools.partial(layer_kernel, n_req, n_tp), out_shape=tu...  21.8 us
    pallas_call x1, Pallas kernels, shards(): pl.pallas_call(store_kernel, out_shape=tuple((jax.ShapeDtypeStruct(shape,...  0.86 us

profile of v5, /device:TPU:14, one launch (start us, length us, event | category | flops | bytes accessed | tf_op | source)
XLA Modules:
  0.0 23.9 jit_solution(4239805997092242648)
XLA Ops:
  1.3 21.8 %decode_layer.1 = (bf16[16,2048]{1,0:T(8,128)(2,1)S(1)}, bf16[16,2048]{1,0:T(8,128)(2,1)S(1)}, bf16[10,64,512]{2,1,0:T(8,128)(2,1)S(1)}) custom-call(s32[2,24]{1,0:T(2,128)} %prompt_table_hbm.1, s32[2]{0:T(128)} %prompt_len_hbm.1, s32[16]{0:T(128)} %req_group_hbm.1, s32[2,16]{1,0:T(2,128)} %bitcast.4, s32[16]{0:T(128)} %cont_len_hbm.1, s32[2,6]{1,0:T(2,128)} %bitcast.5, ...), custom_call_target="tpu_custom_call" | custom-call | tf_op jit(solution)/shard_map/decode_layer/pallas_call | solution.py:433
  23.1 0.9 %store_results.1 = (bf16[16,2048]{1,0:T(8,128)(2,1)}, bf16[16,2048]{1,0:T(8,128)(2,1)}, bf16[8,64,512]{2,1,0:T(8,128)(2,1)}) custom-call(bf16[16,2048]{1,0:T(8,128)(2,1)S(1)} %get-tuple-element.6.refs_0_, bf16[16,2048]{1,0:T(8,128)(2,1)S(1)} %get-tuple-element.7.refs_1_, bf16[10,64,512]{2,1,0:T(8,128)(2,1)S(1)} %get-tuple-element.8.refs_2_), custom_call_target="tpu_custom_call" | custom-call | tf_op jit(solution)/shard_map/store_results/pallas_call | solution.py:461

commit v6 on v5

--- a/solution.py
+++ b/solution.py
@@ -13,7 +13,7 @@
 RELAYS = MIG_CAP
 ROW = 4
 CONT_PAGES = 2
-POOL_CHUNKS = 5
+POOL_CHUNKS = 2
 MESH = pl.DeviceIdType.MESH
 F32 = jnp.float32
 BF16 = jnp.bfloat16
@@ -96,8 +96,6 @@
         pltpu.make_async_copy(source, target, small_sem.at[index])
         for index, (source, target) in enumerate(tables)
     ]
-    for copy in small_copies[:4]:
-        copy.start()
     per_chunk = pages // POOL_CHUNKS
     pool_copies = []
     for chunk in range(POOL_CHUNKS):
@@ -107,7 +105,7 @@
         )
         pool_copies[-1].start()
     weight_copy = pltpu.make_async_copy(weight_hbm, weight, weight_sem)
-    for copy in small_copies[4:]:
+    for copy in small_copies:
         copy.start()
 
     barrier = pltpu.get_barrier_semaphore()
@@ -122,8 +120,13 @@
     def req_at(step):
         return lax.rem(my_req + n_req + step, n_req)
 
+    def swapped(index):
+        return index + 1 - 2 * lax.rem(index, 2)
+
+    turn_of = swapped(my_tp)
+
     def tp_at(step):
-        return lax.rem(my_tp + n_tp + step, n_tp)
+        return swapped(lax.rem(turn_of + n_tp + step, n_tp))
 
     for offset in range(1, MIG_REACH + 1):
         crosses = my_y < offset
@@ -133,7 +136,7 @@
     for step in range(1, ROW):
         pl.when(my_y + step < ROW)(functools.partial(tell, barrier, "req", req_at(step)))
     for step in range(1, n_tp):
-        pl.when(my_tp + step < n_tp)(functools.partial(tell, barrier, "tp", tp_at(step)))
+        pl.when(turn_of + step < n_tp)(functools.partial(tell, barrier, "tp", tp_at(step)))
 
     for copy in small_copies[:4]:
         copy.wait()
@@ -151,13 +154,13 @@
     weight_copy.start()
 
     def send_pages():
-        pl.semaphore_wait(barrier, 2 * my_y + 1 - far + my_tp)
+        pl.semaphore_wait(barrier, 2 * my_y + 1 - far + turn_of)
         for step in range(1, ROW):
             pl.when(my_y >= step)(
                 functools.partial(tell, ready.at[0], "req", req_at(-step))
             )
         for step in range(1, n_tp):
-            pl.when(my_tp >= step)(
+            pl.when(turn_of >= step)(
                 functools.partial(tell, ready.at[1], "tp", tp_at(-step))
             )
         first = MIG_CAP * (ROW - 1 - my_y)
@@ -308,9 +311,9 @@
         return pl.ds(pl.multiple_of(index * block, block), block)
 
 
-    @pl.when(my_tp < n_tp - 1)
+    @pl.when(turn_of < n_tp - 1)
     def _():
-        pl.semaphore_wait(ready.at[1], n_tp - 1 - my_tp)
+        pl.semaphore_wait(ready.at[1], n_tp - 1 - turn_of)
 
     sum_copies = []
     for step in (4, 3, 5, 2, 6, 1, 7):
@@ -378,11 +381,13 @@
     count = len(refs) // 2
     copies = [
         pltpu.make_async_copy(
-            refs[index].at[pl.ds(0, refs[count + index].shape[0])],
-            refs[count + index],
+            refs[index].at[pl.ds(start, step)],
+            refs[count + index].at[pl.ds(start, step)],
             refs[-1].at[index],
         )
         for index in range(count)
+        for step in [refs[count + index].shape[0] // (4 if index == count - 1 else 1)]
+        for start in range(0, refs[count + index].shape[0], step)
     ]
     for copy in copies:
         copy.start()

time: 24.1 us -> 24 us (level)
  no operation moved by 1% of the time
where the time goes in v6:
time: 24 us; the launch traced here: 23.9 us
  Pallas kernels  22.6 us (94%)
  between operations  1.29 us (5%)
    pallas_call x1, Pallas kernels, shards(): pl.pallas_call(functools.partial(layer_kernel, n_req, n_tp), out_shape=tu...  21.7 us
    pallas_call x1, Pallas kernels, shards(): pl.pallas_call(store_kernel, out_shape=tuple((jax.ShapeDtypeStruct(shape,...  0.85 us

profile of v6, /device:TPU:14, one launch (start us, length us, event | category | flops | bytes accessed | tf_op | source)
XLA Modules:
  0.0 23.9 jit_solution(18179086707023736661)
XLA Ops:
  1.3 21.7 %decode_layer.1 = (bf16[16,2048]{1,0:T(8,128)(2,1)S(1)}, bf16[16,2048]{1,0:T(8,128)(2,1)S(1)}, bf16[10,64,512]{2,1,0:T(8,128)(2,1)S(1)}) custom-call(s32[2,24]{1,0:T(2,128)} %prompt_table_hbm.1, s32[2]{0:T(128)} %prompt_len_hbm.1, s32[16]{0:T(128)} %req_group_hbm.1, s32[2,16]{1,0:T(2,128)} %bitcast.4, s32[16]{0:T(128)} %cont_len_hbm.1, s32[2,6]{1,0:T(2,128)} %bitcast.5, ...), custom_call_target="tpu_custom_call" | custom-call | tf_op jit(solution)/shard_map/decode_layer/pallas_call | solution.py:438
  23.0 0.9 %store_results.1 = (bf16[16,2048]{1,0:T(8,128)(2,1)}, bf16[16,2048]{1,0:T(8,128)(2,1)}, bf16[8,64,512]{2,1,0:T(8,128)(2,1)}) custom-call(bf16[16,2048]{1,0:T(8,128)(2,1)S(1)} %get-tuple-element.6.refs_0_, bf16[16,2048]{1,0:T(8,128)(2,1)S(1)} %get-tuple-element.7.refs_1_, bf16[10,64,512]{2,1,0:T(8,128)(2,1)S(1)} %get-tuple-element.8.refs_2_), custom_call_target="tpu_custom_call" | custom-call | tf_op jit(solution)/shard_map/store_results/pallas_call | solution.py:466

commit v7 on v6

--- a/solution.py
+++ b/solution.py
@@ -13,7 +13,7 @@
 RELAYS = MIG_CAP
 ROW = 4
 CONT_PAGES = 2
-POOL_CHUNKS = 2
+POOL_CHUNKS = 1
 MESH = pl.DeviceIdType.MESH
 F32 = jnp.float32
 BF16 = jnp.bfloat16

time: 24 us -> 24.1 us (level)
  no operation moved by 1% of the time
where the time goes in v7:
time: 24.1 us; the launch traced here: 23.9 us
  Pallas kernels  22.6 us (94%)
  between operations  1.29 us (5%)
    pallas_call x1, Pallas kernels, shards(): pl.pallas_call(functools.partial(layer_kernel, n_req, n_tp), out_shape=tu...  21.8 us
    pallas_call x1, Pallas kernels, shards(): pl.pallas_call(store_kernel, out_shape=tuple((jax.ShapeDtypeStruct(shape,...  0.85 us

profile of v7, /device:TPU:14, one launch (start us, length us, event | category | flops | bytes accessed | tf_op | source)
XLA Modules:
  0.0 23.9 jit_solution(2145998739560431027)
XLA Ops:
  1.3 21.8 %decode_layer.1 = (bf16[16,2048]{1,0:T(8,128)(2,1)S(1)}, bf16[16,2048]{1,0:T(8,128)(2,1)S(1)}, bf16[10,64,512]{2,1,0:T(8,128)(2,1)S(1)}) custom-call(s32[2,24]{1,0:T(2,128)} %prompt_table_hbm.1, s32[2]{0:T(128)} %prompt_len_hbm.1, s32[16]{0:T(128)} %req_group_hbm.1, s32[2,16]{1,0:T(2,128)} %bitcast.4, s32[16]{0:T(128)} %cont_len_hbm.1, s32[2,6]{1,0:T(2,128)} %bitcast.5, ...), custom_call_target="tpu_custom_call" | custom-call | tf_op jit(solution)/shard_map/decode_layer/pallas_call | solution.py:438
  23.0 0.9 %store_results.1 = (bf16[16,2048]{1,0:T(8,128)(2,1)}, bf16[16,2048]{1,0:T(8,128)(2,1)}, bf16[8,64,512]{2,1,0:T(8,128)(2,1)}) custom-call(bf16[16,2048]{1,0:T(8,128)(2,1)S(1)} %get-tuple-element.6.refs_0_, bf16[16,2048]{1,0:T(8,128)(2,1)S(1)} %get-tuple-element.7.refs_1_, bf16[10,64,512]{2,1,0:T(8,128)(2,1)S(1)} %get-tuple-element.8.refs_2_), custom_call_target="tpu_custom_call" | custom-call | tf_op jit(solution)/shard_map/store_results/pallas_call | solution.py:466
